TPU v7x, 32 devices: a whole 2x2x4 slice. The times are simulated.
32 devices in a mesh: gx: 2 (over y), gy: 4 (over x, core), gz: 4 (over z).
Axes of the slice: x: 2, y: 2, z: 4, core: 2. Of those that a mesh axis runs over, the one named last changes fastest.
Arguments:
- wavefunctions: bfloat16 [32, 64, 64, 128], P('gx', 'gy', 'gz'), may hold values from -512 to 512, as said below
- potential: float32 [32, 64, 64], P('gx', 'gy', 'gz'), may hold values from 0 to 3
Outputs:
- rotated: float32 [32, 64, 64, 128], P('gx', 'gy', 'gz')
- residual: bfloat16 [32, 64, 64, 128], P('gx', 'gy', 'gz')
- quotients: float32 [128], replicated
- norms: float32 [128], replicated
Inputs may be any that keep to these rules, and one draw needn't show every extreme that they name: `wavefunctions`: real values mixed across bands, of full rank.
All inputs are finite; a program needn't handle non-finite values.
Results may differ from a plain program's by a relative error of at most 0.0007.
Values may be sent and summed in bfloat16 or wider, within the bound.
A program may use at most 64 MiB of HBM per device.

v0:
```python
import jax
import jax.numpy as jnp
from jax import lax
from jax.sharding import PartitionSpec as P


def extended(block, sides, width):
    for axis, dim in sides:
        count = lax.axis_size(axis)
        forward = [(i, i + 1) for i in range(count - 1)]
        forward.append((count - 1, 0))
        backward = [(target, source) for source, target in forward]
        low = lax.ppermute(
            lax.slice_in_dim(block, block.shape[dim] - width, None, axis=dim), axis, forward
        )
        high = lax.ppermute(lax.slice_in_dim(block, 0, width, axis=dim), axis, backward)
        block = jnp.concatenate([low, block, high], axis=dim)
    return block


def stencil(padded, center, potential):
    cx, cy, cz = (center.shape[0], center.shape[1], center.shape[2])
    total = -30.0 * 3.0 * center
    weights = ((0, -1.0), (1, 16.0), (3, 16.0), (4, -1.0))
    for offset, weight in weights:
        total = total + weight * padded[offset : offset + cx, 2 : 2 + cy, 2 : 2 + cz]
        total = total + weight * padded[2 : 2 + cx, offset : offset + cy, 2 : 2 + cz]
        total = total + weight * padded[2 : 2 + cx, 2 : 2 + cy, offset : offset + cz]
    return -0.5 * total / 12.0 + potential[..., None] * center


def rotate(field, inverse):
    shape = field.shape
    flat = field.reshape(-1, shape[3])
    return jnp.dot(flat, inverse.T, precision=lax.Precision.HIGHEST).reshape(shape)


def local(wavefunctions, potential):
    cx, cy, cz, bands = wavefunctions.shape
    total_cells = cx * cy * cz * lax.axis_size("gx") * lax.axis_size("gy") * lax.axis_size("gz")
    flat = wavefunctions.reshape(-1, bands)
    local_correlation = lax.dot_general(
        flat, flat, (((0,), (0,)), ((), ())), preferred_element_type=jnp.float32
    )
    correlation = lax.psum(local_correlation, ("gx", "gy", "gz")) / total_cells
    factor = jnp.linalg.cholesky(correlation)
    inverse = lax.linalg.triangular_solve(
        factor, jnp.eye(bands, dtype=jnp.float32), left_side=True, lower=True
    )
    given = wavefunctions.astype(jnp.float32)
    rotated = rotate(given, inverse)
    padded = extended(rotated, (("gx", 0), ("gy", 1), ("gz", 2)), 2)
    applied = stencil(padded, rotated, potential)
    cross = jnp.sum(rotated * applied, axis=(0, 1, 2))
    self_applied = jnp.sum(applied * applied, axis=(0, 1, 2))
    self_rotated = jnp.sum(rotated * rotated, axis=(0, 1, 2))
    cross_all, applied_all, rotated_all = lax.psum(
        (cross, self_applied, self_rotated), ("gx", "gy", "gz")
    )
    quotients = cross_all / total_cells
    squares = applied_all - 2.0 * quotients * cross_all + quotients * quotients * rotated_all
    leftover = applied - quotients * rotated
    norms = jnp.sqrt(squares / total_cells + 1e-06)
    return (rotated, leftover.astype(jnp.bfloat16), quotients, norms)


def solution(mesh):
    placed = (P("gx", "gy", "gz", None), P("gx", "gy", "gz"))
    return jax.shard_map(
        local,
        mesh=mesh,
        in_specs=placed,
        out_specs=(P("gx", "gy", "gz", None), P("gx", "gy", "gz", None), P(), P()),
        check_vma=False,
    )
```

profile of v0, /device:TPU:0, one launch (start us, length us, event | category | flops | bytes accessed | tf_op | source)
XLA Modules:
  0.0 271.0 jit_solution(13407734252116796372)
XLA Ops:
  7.2 1.2 copy-done
  8.4 1.1 convolution_bitcast_fusion.1
  9.5 126.7 %all-reduce.3.cloned.1.call-done = f32[128,128]{0,1:T(8,128)} async-done(((f32[128,128]{0,1:T(8,128)}), f32[128,128]{0,1:T(8,128)}) %all-reduce.3.cloned.1.call-update) | async-done | bytes 65552 | tf_op jit(solution)/shard_map/psum | solution.py:45
  136.3 0.8 broadcast_multiply_fusion
  137.2 0.9 fusion.25
  138.1 11.7 %cholesky.17 = f32[128,128]{1,0:T(8,128)S(1)} custom-call(f32[128,128]{1,0:T(8,128)S(1)} %fusion.25), custom_call_target="Cholesky" | custom-call | tf_op jit(solution)/shard_map/jit(cholesky)/cholesky | solution.py:46
  151.1 9.8 %custom-call.6 = f32[1,128,128]{1,2,0:T(8,128)S(1)} custom-call(f32[1,128,128]{2,1,0:T(8,128)S(1)} %fusion.22), custom_call_target="InvertDiagBlocksLowerTriangular" | custom-call | tf_op jit(solution)/shard_map/triangular_solve | solution.py:47
  161.2 1.1 multiply_reduce_fusion
  162.3 1.3 copy-done.2
  165.3 1.5 collective-permute-start.1
  167.4 1.9 copy.20
  169.3 4.7 %collective-permute-done.1 = f32[2,16,16,128]{3,2,1,0:T(8,128)S(1)} collective-permute-done((f32[2,16,16,128]{3,2,1,0:T(8,128)}, f32[2,16,16,128]{3,2,1,0:T(8,128)S(1)}, u32[]{:S(2)}, u32[]{:S(2)}) %collective-permute-start.1) | collective-permute-done | bytes 262176 | tf_op jit(solution)/shard_map/ppermute | solution.py:16
  174.0 5.7 %collective-permute-done = f32[2,16,16,128]{3,2,1,0:T(8,128)} collective-permute-done((f32[2,16,16,128]{3,2,1,0:T(8,128)}, f32[2,16,16,128]{3,2,1,0:T(8,128)}, u32[]{:S(2)}, u32[]{:S(2)}) %collective-permute-start) | collective-permute-done | bytes 262176 | tf_op jit(solution)/shard_map/ppermute | solution.py:13
  181.2 1.2 collective-permute-start.3
  182.3 6.5 %collective-permute-done.2 = f32[20,2,16,128]{3,2,1,0:T(8,128)S(1)} collective-permute-done((f32[20,2,16,128]{3,2,1,0:T(8,128)S(1)}, f32[20,2,16,128]{3,2,1,0:T(8,128)S(1)}, u32[]{:S(2)}, u32[]{:S(2)}) %collective-permute-start.2) | collective-permute-done | bytes 327712 | tf_op jit(solution)/shard_map/ppermute | solution.py:13
  189.6 1.3 pad_maximum_fusion.17
  190.8 1.2 collective-permute-start.4
  192.0 2.7 %collective-permute-start.5 = (f32[20,20,2,128]{3,2,1,0:T(2,128)S(1)}, f32[20,20,2,128]{3,2,1,0:T(2,128)S(1)}, u32[]{:S(2)}, u32[]{:S(2)}) collective-permute-start(f32[20,20,2,128]{3,2,1,0:T(2,128)S(1)} %get-tuple-element.17), channel_id=1, source_target_pairs={{1,0},{2,1},{3,2},{0,3},{5,4},{6,5},{7,6},{4,7},{9,8},{10,9},{11,1... | collective-permute-start | bytes 1228808 | tf_op jit(solution)/shard_map/ppermute | solution.py:16
  194.7 1.6 maximum_maximum_fusion
  196.4 8.7 %collective-permute-done.4 = f32[20,20,2,128]{3,2,1,0:T(2,128)S(1)} collective-permute-done((f32[20,20,2,128]{3,2,1,0:T(2,128)S(1)}, f32[20,20,2,128]{3,2,1,0:T(2,128)S(1)}, u32[]{:S(2)}, u32[]{:S(2)}) %collective-permute-start.4) | collective-permute-done | bytes 409632 | tf_op jit(solution)/shard_map/ppermute | solution.py:13
  205.1 7.6 %collective-permute-done.5 = f32[20,20,2,128]{3,2,1,0:T(2,128)S(1)} collective-permute-done((f32[20,20,2,128]{3,2,1,0:T(2,128)S(1)}, f32[20,20,2,128]{3,2,1,0:T(2,128)S(1)}, u32[]{:S(2)}, u32[]{:S(2)}) %collective-permute-start.5) | collective-permute-done | bytes 409632 | tf_op jit(solution)/shard_map/ppermute | solution.py:16
  212.7 8.0 %multiply_reduce_fusion.1 = (f32[128]{0:T(128)S(1)}, f32[128]{0:T(128)S(1)}, f32[16,16,16,128]{3,2,1,0:T(8,128)}) fusion(f32[16,16,16,128]{3,2,1,0:T(8,128)S(1)} %bitcast.26, f32[16,16,16]{2,1,0:T(8,128)S(1)} %copy-done.3, f32[20,20,2,128]{3,2,1,0:T(2,128)S(1)} %collective-permute-done.5, f32[20,2,16,128]{3,2,1,0:T(8,128)S(1)} %collective-permute-done.3, ...), kind=kLoop, calls=%fused_computation.48 | loop fusion | flops 29359872 | bytes 14599168 | tf_op jit(solution)/shard_map/reduce_sum | solution.py:55
  220.7 40.1 %all-reduce = (f32[128]{0:T(128)S(1)}, f32[128]{0:T(128)S(1)}, f32[128]{0:T(128)S(1)}) all-reduce(f32[128]{0:T(128)S(1)} %get-tuple-element.9, f32[128]{0:T(128)S(1)} %get-tuple-element.24, f32[128]{0:T(128)S(1)} %get-tuple-element.8), channel_id=1, replica_groups=mesh['gx'=2,'gy'=4,'gz'=4] {'gx','gy','gz'}, use_global_device_ids=true, to_apply=%region_4.5 | all-reduce | flops 384 | bytes 3072 | tf_op jit(solution)/shard_map/psum | solution.py:57
  261.3 2.8 %subtract_convert_fusion = bf16[16,16,16,128]{3,2,1,0:T(8,128)(2,1)} fusion(f32[16,16,16,128]{3,2,1,0:T(8,128)} %get-tuple-element.15, f32[128]{0:T(128)S(1)} %get-tuple-element.14, f32[4096,128]{1,0:T(8,128)S(1)} %copy.20), kind=kLoop, calls=%fused_computation.49 | loop fusion | flops 1572864 | bytes 5243392 | tf_op jit(solution)/shard_map/convert_element_type | solution.py:64
  (23 shorter events, 6.7 us)
Async XLA Ops:
  7.2 1.2 copy-start
  7.2 129.1 %all-reduce.3.cloned.1.call-start = ((), (), s32[]{:S(2)}) async-start(), calls=%async_computation | async-start | bytes 131072 | tf_op jit(solution)/shard_map/psum | solution.py:45
  162.3 1.3 copy-start.2
  165.3 8.6 %collective-permute-start.1 = (f32[2,16,16,128]{3,2,1,0:T(8,128)}, f32[2,16,16,128]{3,2,1,0:T(8,128)S(1)}, u32[]{:S(2)}, u32[]{:S(2)}) collective-permute-start(f32[2,16,16,128]{3,2,1,0:T(8,128)} %bitcast.8), channel_id=1, source_target_pairs={{16,0},{0,16},{17,1},{1,17},{18,2},{2,18},{19,3},{3,19},{20,4},{4,... | collective-permute-start | bytes 786440 | tf_op jit(solution)/shard_map/ppermute | solution.py:16
  166.8 12.9 %collective-permute-start = (f32[2,16,16,128]{3,2,1,0:T(8,128)}, f32[2,16,16,128]{3,2,1,0:T(8,128)}, u32[]{:S(2)}, u32[]{:S(2)}) collective-permute-start(f32[2,16,16,128]{3,2,1,0:T(8,128)} %bitcast.7), channel_id=1, source_target_pairs={{0,16},{16,0},{1,17},{17,1},{2,18},{18,2},{3,19},{19,3},{4,20},{20... | collective-permute-start | bytes 786440 | tf_op jit(solution)/shard_map/ppermute | solution.py:13
  169.3 92.0 %copy-start.1 = (f32[4096,128]{1,0:T(8,128)}, f32[4096,128]{1,0:T(8,128)S(1)}, u32[]{:S(2)}) copy-start(f32[4096,128]{1,0:T(8,128)S(1)} %copy.20) | copy-start | bytes 6291460
  180.5 8.3 %collective-permute-start.2 = (f32[20,2,16,128]{3,2,1,0:T(8,128)S(1)}, f32[20,2,16,128]{3,2,1,0:T(8,128)S(1)}, u32[]{:S(2)}, u32[]{:S(2)}) collective-permute-start(f32[20,2,16,128]{3,2,1,0:T(8,128)S(1)} %get-tuple-element.20), channel_id=1, source_target_pairs={{0,4},{4,8},{8,12},{12,0},{1,5},{5,9},{9,13},{13,1},{2,6},{6,10},{... | collective-permute-start | bytes 983048 | tf_op jit(solution)/shard_map/ppermute | solution.py:13
  181.2 8.4 %collective-permute-start.3 = (f32[20,2,16,128]{3,2,1,0:T(8,128)S(1)}, f32[20,2,16,128]{3,2,1,0:T(8,128)S(1)}, u32[]{:S(2)}, u32[]{:S(2)}) collective-permute-start(f32[20,2,16,128]{3,2,1,0:T(8,128)S(1)} %get-tuple-element.21), channel_id=1, source_target_pairs={{4,0},{8,4},{12,8},{0,12},{5,1},{9,5},{13,9},{1,13},{6,2},{10,6},{... | collective-permute-start | bytes 983048 | tf_op jit(solution)/shard_map/ppermute | solution.py:16
  190.8 14.2 %collective-permute-start.4 = (f32[20,20,2,128]{3,2,1,0:T(2,128)S(1)}, f32[20,20,2,128]{3,2,1,0:T(2,128)S(1)}, u32[]{:S(2)}, u32[]{:S(2)}) collective-permute-start(f32[20,20,2,128]{3,2,1,0:T(2,128)S(1)} %get-tuple-element.16), channel_id=1, source_target_pairs={{0,1},{1,2},{2,3},{3,0},{4,5},{5,6},{6,7},{7,4},{8,9},{9,10},{10,1... | collective-permute-start | bytes 1228808 | tf_op jit(solution)/shard_map/ppermute | solution.py:13
  192.0 20.7 %copy-start.3 = (f32[16,16,16]{2,1,0:T(8,128)S(1)}, f32[16,16,16]{2,1,0:T(8,128)}, u32[]{:S(2)}) copy-start(f32[16,16,16]{2,1,0:T(8,128)} %param.3) | copy-start | bytes 49156
  192.0 20.7 %collective-permute-start.5 = (f32[20,20,2,128]{3,2,1,0:T(2,128)S(1)}, f32[20,20,2,128]{3,2,1,0:T(2,128)S(1)}, u32[]{:S(2)}, u32[]{:S(2)}) collective-permute-start(f32[20,20,2,128]{3,2,1,0:T(2,128)S(1)} %get-tuple-element.17), channel_id=1, source_target_pairs={{1,0},{2,1},{3,2},{0,3},{5,4},{6,5},{7,6},{4,7},{9,8},{10,9},{11,1... | collective-permute-start | bytes 1228808 | tf_op jit(solution)/shard_map/ppermute | solution.py:16
  261.3 2.9 %copy-start.4 = (f32[128]{0:T(128)}, f32[128]{0:T(128)S(1)}, u32[]{:S(2)}) copy-start(f32[128]{0:T(128)S(1)} %get-tuple-element.14) | copy-start | bytes 1540
Sparse Core Ops, SparseCore 0:
  14.1 122.0 all-reduce.2
where the time goes:
time: 272 us; the launch traced here: 271 us
  waiting for transfers between devices  161 us (59%)
  blocking collectives  40.1 us (15%)
  other arithmetic  39.7 us (15%)
  between operations  14.1 us (5%)
  starting transfers between devices  7.74 us (3%)
  local copies, waits for them, and re-layouts  6.19 us (2%)
    psum x1, waiting for transfers between devices, local(): correlation = lax.psum(local_correlation, ('gx', 'gy', 'gz')) / total_cells  127 us
    psum x1, blocking collectives, local(): lax.psum((cross, self_applied, self_rotated), ('gx', 'gy', 'gz'))  40.1 us
    ppermute x3, waiting for transfers between devices, extended(): lax.ppermute(lax.slice_in_dim(block, block.shape[dim] - width, None, axis...  20.9 us
    ppermute x3, waiting for transfers between devices, extended(): lax.ppermute(lax.slice_in_dim(block, 0, width, axis=dim), axis, backward)  13.1 us
    another operation x3, other arithmetic, local(): factor = jnp.linalg.cholesky(correlation)  12.4 us
    another operation x2, other arithmetic, local(): lax.linalg.triangular_solve(factor, jnp.eye(bands, dtype=jnp.float32), le...  10.5 us
    reduce_sum x1, other arithmetic, local(): self_applied = jnp.sum(applied * applied, axis=(0, 1, 2))  8.02 us
  transfers between devices with their start and end apart: 7, of which 7 were waited for; matrix products, arithmetic and copies ran while one was open for 1% of the time, Pallas kernels for 0%

commit v1 on v0

--- a/solution.py
+++ b/solution.py
@@ -42,7 +42,9 @@
     local_correlation = lax.dot_general(
         flat, flat, (((0,), (0,)), ((), ())), preferred_element_type=jnp.float32
     )
-    correlation = lax.psum(local_correlation, ("gx", "gy", "gz")) / total_cells
+    correlation = (
+        jnp.sum(lax.all_gather(local_correlation, ("gx", "gy", "gz")), axis=0) / total_cells
+    )
     factor = jnp.linalg.cholesky(correlation)
     inverse = lax.linalg.triangular_solve(
         factor, jnp.eye(bands, dtype=jnp.float32), left_side=True, lower=True

time: 272 us -> 204 us (0.75)
  waiting for transfers between devices: 161 us -> 94.5 us
    psum x1 -> x0, waiting for transfers between devices: 127 us -> none  [local(): correlation = lax.psum(local_correlation, ('gx', 'gy', 'gz')) / total_cells]
    all_gather x0 -> x1, waiting for transfers between devices: none -> 61.1 us  [local(): lax.all_gather(local_correlation, ('gx', 'gy', 'gz'))]
  transfers between devices with their start and end apart: 7 -> 7, of which waited for: 7 -> 7; matrix products, arithmetic and copies ran while one was open for 1% -> 2% of each run, Pallas kernels for 0% -> 0%
where the time goes in v1:
time: 204 us
  waiting for transfers between devices  94.5 us (46%)
  other arithmetic  39.7 us (19%)
  blocking collectives  39 us (19%)
  between operations  14.1 us (7%)
  starting transfers between devices  7.73 us (4%)
  local copies, waits for them, and re-layouts  6.19 us (3%)
  matrix products  2.48 us (1%)
    all_gather x1, waiting for transfers between devices, local(): lax.all_gather(local_correlation, ('gx', 'gy', 'gz'))  61.1 us
    psum x1, blocking collectives, local(): lax.psum((cross, self_applied, self_rotated), ('gx', 'gy', 'gz'))  39 us
    ppermute x3, waiting for transfers between devices, extended(): lax.ppermute(lax.slice_in_dim(block, block.shape[dim] - width, None, axis...  20.2 us
    ppermute x3, waiting for transfers between devices, extended(): lax.ppermute(lax.slice_in_dim(block, 0, width, axis=dim), axis, backward)  13.2 us
    another operation x3, other arithmetic, local(): factor = jnp.linalg.cholesky(correlation)  12.4 us
    another operation x2, other arithmetic, local(): lax.linalg.triangular_solve(factor, jnp.eye(bands, dtype=jnp.float32), le...  10.5 us
    reduce_sum x1, other arithmetic, local(): self_applied = jnp.sum(applied * applied, axis=(0, 1, 2))  8.02 us
    ppermute x3, starting transfers between devices, extended(): lax.ppermute(lax.slice_in_dim(block, 0, width, axis=dim), axis, backward)  6.49 us
  transfers between devices with their start and end apart: 7, of which 7 were waited for; matrix products, arithmetic and copies ran while one was open for 2% of the time, Pallas kernels for 0%

profile of v1, /device:TPU:0, one launch (start us, length us, event | category | flops | bytes accessed | tf_op | source)
XLA Modules:
  0.0 203.7 jit_solution(8668996563315974278)
XLA Ops:
  7.2 1.2 copy-done
  8.4 1.1 convolution_bitcast_fusion.1
  9.5 61.1 %all-gather.3.cloned.1.call-done = f32[4096,128]{1,0:T(8,128)} async-done(((f32[128,128]{1,0:T(8,128)}), f32[4096,128]{1,0:T(8,128)}) %all-gather.3.cloned.1.call-update) | async-done | bytes 2097168 | tf_op jit(solution)/shard_map/all_gather | solution.py:46
  70.6 1.7 reduce_sum.38
  72.4 11.7 %cholesky.17 = f32[128,128]{1,0:T(8,128)S(1)} custom-call(f32[128,128]{1,0:T(8,128)S(1)} %fusion.25), custom_call_target="Cholesky" | custom-call | tf_op jit(solution)/shard_map/jit(cholesky)/cholesky | solution.py:48
  85.5 9.8 %custom-call.6 = f32[1,128,128]{1,2,0:T(8,128)S(1)} custom-call(f32[1,128,128]{2,1,0:T(8,128)S(1)} %fusion.22), custom_call_target="InvertDiagBlocksLowerTriangular" | custom-call | tf_op jit(solution)/shard_map/triangular_solve | solution.py:49
  95.5 1.1 multiply_reduce_fusion
  96.7 1.3 copy-done.2
  98.0 0.8 copy.23
  98.9 0.8 copy.24
  99.7 1.5 collective-permute-start.1
  101.7 1.9 copy.22
  103.6 5.4 %collective-permute-done.1 = f32[2,16,16,128]{3,2,1,0:T(8,128)S(1)} collective-permute-done((f32[2,16,16,128]{3,2,1,0:T(8,128)}, f32[2,16,16,128]{3,2,1,0:T(8,128)S(1)}, u32[]{:S(2)}, u32[]{:S(2)}) %collective-permute-start.1) | collective-permute-done | bytes 262176 | tf_op jit(solution)/shard_map/ppermute | solution.py:16
  109.1 5.0 %collective-permute-done = f32[2,16,16,128]{3,2,1,0:T(8,128)} collective-permute-done((f32[2,16,16,128]{3,2,1,0:T(8,128)}, f32[2,16,16,128]{3,2,1,0:T(8,128)}, u32[]{:S(2)}, u32[]{:S(2)}) %collective-permute-start) | collective-permute-done | bytes 262176 | tf_op jit(solution)/shard_map/ppermute | solution.py:13
  114.9 1.7 collective-permute-start.3
  116.7 6.5 %collective-permute-done.2 = f32[20,2,16,128]{3,2,1,0:T(8,128)S(1)} collective-permute-done((f32[20,2,16,128]{3,2,1,0:T(8,128)S(1)}, f32[20,2,16,128]{3,2,1,0:T(8,128)S(1)}, u32[]{:S(2)}, u32[]{:S(2)}) %collective-permute-start.2) | collective-permute-done | bytes 327712 | tf_op jit(solution)/shard_map/ppermute | solution.py:13
  123.9 1.3 pad_maximum_fusion.17
  125.7 3.3 %collective-permute-start.5 = (f32[20,20,2,128]{3,2,1,0:T(2,128)S(1)}, f32[20,20,2,128]{3,2,1,0:T(2,128)S(1)}, u32[]{:S(2)}, u32[]{:S(2)}) collective-permute-start(f32[20,20,2,128]{3,2,1,0:T(2,128)S(1)} %get-tuple-element.17), channel_id=1, source_target_pairs={{1,0},{2,1},{3,2},{0,3},{5,4},{6,5},{7,6},{4,7},{9,8},{10,9},{11,1... | collective-permute-start | bytes 1228808 | tf_op jit(solution)/shard_map/ppermute | solution.py:16
  129.0 1.6 maximum_maximum_fusion
  130.7 8.7 %collective-permute-done.4 = f32[20,20,2,128]{3,2,1,0:T(2,128)S(1)} collective-permute-done((f32[20,20,2,128]{3,2,1,0:T(2,128)S(1)}, f32[20,20,2,128]{3,2,1,0:T(2,128)S(1)}, u32[]{:S(2)}, u32[]{:S(2)}) %collective-permute-start.4) | collective-permute-done | bytes 409632 | tf_op jit(solution)/shard_map/ppermute | solution.py:13
  139.4 7.1 %collective-permute-done.5 = f32[20,20,2,128]{3,2,1,0:T(2,128)S(1)} collective-permute-done((f32[20,20,2,128]{3,2,1,0:T(2,128)S(1)}, f32[20,20,2,128]{3,2,1,0:T(2,128)S(1)}, u32[]{:S(2)}, u32[]{:S(2)}) %collective-permute-start.5) | collective-permute-done | bytes 409632 | tf_op jit(solution)/shard_map/ppermute | solution.py:16
  146.5 8.0 %multiply_reduce_fusion.1 = (f32[128]{0:T(128)S(1)}, f32[128]{0:T(128)S(1)}, f32[16,16,16,128]{3,2,1,0:T(8,128)}) fusion(f32[16,16,16,128]{3,2,1,0:T(8,128)S(1)} %bitcast.29, f32[16,16,16]{2,1,0:T(8,128)S(1)} %copy-done.3, f32[20,20,2,128]{3,2,1,0:T(2,128)S(1)} %collective-permute-done.5, f32[20,2,16,128]{3,2,1,0:T(8,128)S(1)} %collective-permute-done.3, ...), kind=kLoop, calls=%fused_computation.48 | loop fusion | flops 29359872 | bytes 14599168 | tf_op jit(solution)/shard_map/reduce_sum | solution.py:57
  154.5 39.0 %all-reduce = (f32[128]{0:T(128)S(1)}, f32[128]{0:T(128)S(1)}, f32[128]{0:T(128)S(1)}) all-reduce(f32[128]{0:T(128)S(1)} %get-tuple-element.9, f32[128]{0:T(128)S(1)} %get-tuple-element.24, f32[128]{0:T(128)S(1)} %get-tuple-element.8), channel_id=1, replica_groups=mesh['gx'=2,'gy'=4,'gz'=4] {'gx','gy','gz'}, use_global_device_ids=true, to_apply=%region_4.5 | all-reduce | flops 384 | bytes 3072 | tf_op jit(solution)/shard_map/psum | solution.py:59
  194.0 2.8 %subtract_convert_fusion = bf16[16,16,16,128]{3,2,1,0:T(8,128)(2,1)} fusion(f32[16,16,16,128]{3,2,1,0:T(8,128)} %get-tuple-element.15, f32[128]{0:T(128)S(1)} %get-tuple-element.14, f32[4096,128]{1,0:T(8,128)S(1)} %copy.22), kind=kLoop, calls=%fused_computation.49 | loop fusion | flops 1572864 | bytes 5243392 | tf_op jit(solution)/shard_map/convert_element_type | solution.py:66
  (23 shorter events, 5.0 us)
Async XLA Ops:
  7.2 1.2 copy-start
  7.2 63.4 %all-gather.3.cloned.1.call-start = ((), (), s32[]{:S(2)}) async-start(), calls=%async_computation | async-start | bytes 2162688 | tf_op jit(solution)/shard_map/all_gather | solution.py:46
  96.7 1.3 copy-start.2
  99.7 9.4 %collective-permute-start.1 = (f32[2,16,16,128]{3,2,1,0:T(8,128)}, f32[2,16,16,128]{3,2,1,0:T(8,128)S(1)}, u32[]{:S(2)}, u32[]{:S(2)}) collective-permute-start(f32[2,16,16,128]{3,2,1,0:T(8,128)} %bitcast.10), channel_id=1, source_target_pairs={{16,0},{0,16},{17,1},{1,17},{18,2},{2,18},{19,3},{3,19},{20,4},{4,... | collective-permute-start | bytes 786440 | tf_op jit(solution)/shard_map/ppermute | solution.py:16
  101.2 12.9 %collective-permute-start = (f32[2,16,16,128]{3,2,1,0:T(8,128)}, f32[2,16,16,128]{3,2,1,0:T(8,128)}, u32[]{:S(2)}, u32[]{:S(2)}) collective-permute-start(f32[2,16,16,128]{3,2,1,0:T(8,128)} %bitcast.9), channel_id=1, source_target_pairs={{0,16},{16,0},{1,17},{17,1},{2,18},{18,2},{3,19},{19,3},{4,20},{20... | collective-permute-start | bytes 786440 | tf_op jit(solution)/shard_map/ppermute | solution.py:13
  103.6 90.4 %copy-start.1 = (f32[4096,128]{1,0:T(8,128)}, f32[4096,128]{1,0:T(8,128)S(1)}, u32[]{:S(2)}) copy-start(f32[4096,128]{1,0:T(8,128)S(1)} %copy.22) | copy-start | bytes 6291460
  114.9 8.3 %collective-permute-start.2 = (f32[20,2,16,128]{3,2,1,0:T(8,128)S(1)}, f32[20,2,16,128]{3,2,1,0:T(8,128)S(1)}, u32[]{:S(2)}, u32[]{:S(2)}) collective-permute-start(f32[20,2,16,128]{3,2,1,0:T(8,128)S(1)} %get-tuple-element.20), channel_id=1, source_target_pairs={{0,4},{4,8},{8,12},{12,0},{1,5},{5,9},{9,13},{13,1},{2,6},{6,10},{... | collective-permute-start | bytes 983048 | tf_op jit(solution)/shard_map/ppermute | solution.py:13
  114.9 8.9 %collective-permute-start.3 = (f32[20,2,16,128]{3,2,1,0:T(8,128)S(1)}, f32[20,2,16,128]{3,2,1,0:T(8,128)S(1)}, u32[]{:S(2)}, u32[]{:S(2)}) collective-permute-start(f32[20,2,16,128]{3,2,1,0:T(8,128)S(1)} %get-tuple-element.21), channel_id=1, source_target_pairs={{4,0},{8,4},{12,8},{0,12},{5,1},{9,5},{13,9},{1,13},{6,2},{10,6},{... | collective-permute-start | bytes 983048 | tf_op jit(solution)/shard_map/ppermute | solution.py:16
  125.2 14.2 %collective-permute-start.4 = (f32[20,20,2,128]{3,2,1,0:T(2,128)S(1)}, f32[20,20,2,128]{3,2,1,0:T(2,128)S(1)}, u32[]{:S(2)}, u32[]{:S(2)}) collective-permute-start(f32[20,20,2,128]{3,2,1,0:T(2,128)S(1)} %get-tuple-element.16), channel_id=1, source_target_pairs={{0,1},{1,2},{2,3},{3,0},{4,5},{5,6},{6,7},{7,4},{8,9},{9,10},{10,1... | collective-permute-start | bytes 1228808 | tf_op jit(solution)/shard_map/ppermute | solution.py:13
  125.7 20.7 %copy-start.3 = (f32[16,16,16]{2,1,0:T(8,128)S(1)}, f32[16,16,16]{2,1,0:T(8,128)}, u32[]{:S(2)}) copy-start(f32[16,16,16]{2,1,0:T(8,128)} %param.3) | copy-start | bytes 49156
  125.7 20.7 %collective-permute-start.5 = (f32[20,20,2,128]{3,2,1,0:T(2,128)S(1)}, f32[20,20,2,128]{3,2,1,0:T(2,128)S(1)}, u32[]{:S(2)}, u32[]{:S(2)}) collective-permute-start(f32[20,20,2,128]{3,2,1,0:T(2,128)S(1)} %get-tuple-element.17), channel_id=1, source_target_pairs={{1,0},{2,1},{3,2},{0,3},{5,4},{6,5},{7,6},{4,7},{9,8},{10,9},{11,1... | collective-permute-start | bytes 1228808 | tf_op jit(solution)/shard_map/ppermute | solution.py:16
  194.0 2.9 %copy-start.4 = (f32[128]{0:T(128)}, f32[128]{0:T(128)S(1)}, u32[]{:S(2)}) copy-start(f32[128]{0:T(128)S(1)} %get-tuple-element.14) | copy-start | bytes 1540
Sparse Core Ops, SparseCore 0:
  11.5 59.0 all-gather.2
